TPU v7x, 128 devices: a whole 4x4x4 slice. The times are simulated.
128 devices in a mesh: gz: 8 (over x, z_hi), tile: 16 (over z_lo, y, core).
Axes of the slice: x: 4, y: 4, z: 4 (z_hi: 2, z_lo: 2; z = z_hi * 2 + z_lo), core: 2. Of those that a mesh axis runs over, the one named last changes fastest.
Arguments:
- disp: float32 [16, 2, 128, 5120], P('gz', None, 'tile'), may hold values from -6 to 6
- vel: float32 [16, 2, 128, 5120], P('gz', None, 'tile'), may hold values from -4 to 4
- stiff_class: int32 [16, 128, 5120], P('gz', 'tile'), may hold values from 0 to 7
- valid: int32 [16, 128, 5120], P('gz', 'tile'), may hold values 0 or 1
- class_table: float32 [8], replicated, may hold values from 0.3 to 3
- warp: float32 [16, 3, 2], P('gz'), may hold values from 0 to 1
- spring_z: float32 [16, 3], P('gz'), may hold values from 1.2 to 2
- skip_partner: int32 [16], replicated, may hold values from 0 to 15, as said below
Outputs:
- disp_out: float32 [16, 2, 128, 5120], P('gz', None, 'tile')
- vel_out: float32 [16, 2, 128, 5120], P('gz', None, 'tile')
Inputs may be any that keep to these rules, and one draw needn't show every extreme that they name: `skip_partner`: each section's partner lies in another z-block of 2 consecutive sections; the sections of one z-block have at most 1 partners inside any one other z-block, and exactly 1 inside some.
All inputs are finite; a program needn't handle non-finite values. No bound on the sum of `valid` on one device may be relied on, other than what follows from the above.
Results may differ from a plain program's by a relative error of at most 0.0003.
Values sent between devices are 32-bit elements; how exact they have to be, the bound alone decides.
A program may use at most 128 MiB of HBM per device.

v0:
```python
import jax
import jax.numpy as jnp
from jax import lax
from jax.sharding import PartitionSpec as P

ITERS = 3
DAMPING = 0.9
STEP = 0.1


def extended(block, sides, width):
    for axis, dim in sides:
        count = lax.axis_size(axis)
        forward = [(i, i + 1) for i in range(count - 1)]
        backward = [(target, source) for source, target in forward]
        low = lax.ppermute(
            lax.slice_in_dim(block, block.shape[dim] - width, None, axis=dim), axis, forward
        )
        high = lax.ppermute(lax.slice_in_dim(block, 0, width, axis=dim), axis, backward)
        block = jnp.concatenate([low, block, high], axis=dim)
    return block


def shift_left(field):
    return jnp.concatenate([field[..., 1:], jnp.zeros_like(field[..., :1])], axis=-1)


def shift_right(field):
    return jnp.concatenate([jnp.zeros_like(field[..., :1]), field[..., :-1]], axis=-1)


def warped(source, frac_row, frac_col):
    frac_row = frac_row[:, None, None, None]
    frac_col = frac_col[:, None, None, None]
    upper = source[:, :, 1:-1]
    lower = source[:, :, 2:]
    return (
        (1.0 - frac_row) * (1.0 - frac_col) * upper
        + (1.0 - frac_row) * frac_col * shift_left(upper)
        + frac_row * (1.0 - frac_col) * lower
        + frac_row * frac_col * shift_left(lower)
    )


def section_force(
    field_ext, stiff_ext, prev_ext, next_ext, partner_ext, warp, spring_z, has_prev, has_next
):
    center = field_ext[:, :, 1:-1]
    stiff_mid = stiff_ext[:, None, 1:-1]
    stiff_up = stiff_ext[:, None, :-2]
    stiff_down = stiff_ext[:, None, 2:]
    inplane = stiff_mid * (
        stiff_up * (field_ext[:, :, :-2] - center)
        + stiff_down * (field_ext[:, :, 2:] - center)
        + shift_right(stiff_mid) * (shift_right(center) - center)
        + shift_left(stiff_mid) * (shift_left(center) - center)
    )
    pull = (
        spring_z[:, 0][:, None, None, None]
        * has_prev[:, None, None, None]
        * (warped(prev_ext, warp[:, 0, 0], warp[:, 0, 1]) - center)
    )
    pull = pull + spring_z[:, 1][:, None, None, None] * has_next[:, None, None, None] * (
        warped(next_ext, warp[:, 1, 0], warp[:, 1, 1]) - center
    )
    pull = pull + spring_z[:, 2][:, None, None, None] * (
        warped(partner_ext, warp[:, 2, 0], warp[:, 2, 1]) - center
    )
    return inplane + pull


def body(disp, vel, stiff_class, valid, class_table, warp, spring_z, skip_partner):
    local_count = disp.shape[0]
    block_count = lax.axis_size("gz")
    block_index = lax.axis_index("gz")
    total = local_count * block_count
    alive = valid.astype(jnp.float32)
    kappa = jnp.zeros(stiff_class.shape, jnp.float32)
    for level in range(class_table.shape[0]):
        kappa = jnp.where(stiff_class == level, class_table[level], kappa)
    kappa = kappa * alive
    depth = 1
    coeffs = extended(jnp.stack([kappa, alive]), (("tile", 2),), depth)
    global_ids = block_index * local_count + jnp.arange(local_count, dtype=jnp.int32)
    has_prev = (global_ids > 0).astype(jnp.float32)
    has_next = (global_ids < total - 1).astype(jnp.float32)
    wanted = lax.dynamic_slice_in_dim(skip_partner, block_index * local_count, local_count, 0)
    field = disp
    velocity = vel
    for step in range(ITERS):
        field_ext = extended(field, (("tile", 2),), 1)
        vel_inner = velocity
        faces = extended(field_ext, (("gz", 0),), 1)
        piece = lax.all_gather(field_ext, "gz", axis=0, tiled=True)
        count = piece.shape[0]
        inside = (wanted >= 0) & (wanted < count)
        chosen = jnp.take(piece, jnp.clip(wanted, 0, count - 1), axis=0)
        partner_ext = jnp.where(inside[:, None, None, None], chosen, jnp.zeros_like(field_ext))
        force = section_force(
            field_ext,
            coeffs[0],
            faces[:-2],
            faces[2:],
            partner_ext,
            warp,
            spring_z,
            has_prev,
            has_next,
        )
        velocity = coeffs[1][:, None, 1:-1] * (DAMPING * vel_inner + STEP * force)
        field = field_ext[:, :, 1:-1] + STEP * velocity
    return (field, velocity)


def solution(mesh):
    placed = (
        P("gz", None, "tile", None),
        P("gz", None, "tile", None),
        P("gz", "tile", None),
        P("gz", "tile", None),
        P(),
        P("gz", None, None),
        P("gz", None),
        P(),
    )
    return jax.shard_map(
        body,
        mesh=mesh,
        in_specs=placed,
        out_specs=(P("gz", None, "tile", None), P("gz", None, "tile", None)),
        check_vma=False,
    )
```

profile of v0, /device:TPU:0, one launch (start us, length us, event | category | flops | bytes accessed | tf_op | source)
XLA Modules:
  0.0 399.8 jit_solution(12897192505926920959)
XLA Ops:
  7.2 1.4 fusion.111
  8.6 1.3 collective-permute-start.2
  9.9 1.3 collective-permute-start.3
  11.2 1.6 fusion.113
  12.8 6.3 %multiply_bitcast_fusion = f32[1,2,8,5120]{3,2,1,0:T(8,128)S(1)} fusion(s32[2,8,5120]{2,1,0:T(8,128)} %param.13, s32[2,8,5120]{2,1,0:T(8,128)} %param.12, f32[]{:T(128)} %bitcast.7, f32[]{:T(128)} %bitcast.6, f32[]{:T(128)} %bitcast.5, f32[]{:T(128)} %bitcast.4, f32[]{:T(128)} %bitcast.3, f32[]{:T(128)} %bitcast.2, f32[]{:T(128)} %bitcast.1, f32[]{:T(128)} %bitcast), kind=kLoop, calls=%fused_computation.137 | loop fusion | flops 1474560 | bytes 983072 | tf_op jit(solution)/shard_map/stack | solution.py:83
  19.2 1.3 pad_maximum_fusion.4
  20.5 1.5 copy.56
  22.3 5.0 %collective-permute-start = (f32[2,2,1,5120]{3,2,1,0:T(1,128)S(1)}, f32[2,2,1,5120]{3,2,1,0:T(1,128)S(1)}, u32[]{:S(2)}, u32[]{:S(2)}) collective-permute-start(f32[2,2,1,5120]{3,2,1,0:T(1,128)S(1)} %get-tuple-element.70), channel_id=1, source_target_pairs={{0,1},{1,2},{2,3},{3,4},{4,5},{5,6},{6,7},{7,8},{8,9},{9,10},{10,1... | collective-permute-start | bytes 245768 | tf_op jit(solution)/shard_map/ppermute | solution.py:16
  27.2 1.3 collective-permute-start.1
  33.5 1.3 collective-permute-start.5
  34.8 6.4 %collective-permute-start.4 = (f32[1,2,10,5120]{3,1,2,0:T(2,128)S(1)}, f32[1,2,10,5120]{3,1,2,0:T(2,128)S(1)}, u32[]{:S(2)}, u32[]{:S(2)}) collective-permute-start(f32[1,2,10,5120]{3,1,2,0:T(2,128)S(1)} %copy.52), channel_id=1, source_target_pairs={{0,16},{16,32},{32,48},{48,64},{64,80},{80,96},{96,112},{1,17},{17... | collective-permute-start | bytes 1228808 | tf_op jit(solution)/shard_map/ppermute | solution.py:16
  43.3 9.2 %collective-permute-done.5 = f32[1,2,10,5120]{3,1,2,0:T(2,128)S(1)} collective-permute-done((f32[1,2,10,5120]{3,1,2,0:T(2,128)S(1)}, f32[1,2,10,5120]{3,1,2,0:T(2,128)S(1)}, u32[]{:S(2)}, u32[]{:S(2)}) %collective-permute-start.5) | collective-permute-done | bytes 409632 | tf_op jit(solution)/shard_map/ppermute | solution.py:19
  52.7 12.1 %collective-permute-done.4 = f32[1,2,10,5120]{3,1,2,0:T(2,128)S(1)} collective-permute-done((f32[1,2,10,5120]{3,1,2,0:T(2,128)S(1)}, f32[1,2,10,5120]{3,1,2,0:T(2,128)S(1)}, u32[]{:S(2)}, u32[]{:S(2)}) %collective-permute-start.4) | collective-permute-done | bytes 409632 | tf_op jit(solution)/shard_map/ppermute | solution.py:16
  65.3 1.4 copy-done.3
  66.6 2.2 fusion.97
  68.8 67.1 %all-gather.4.cloned.1.call-done = f32[16,2,10,5120]{3,1,2,0:T(2,128)} async-done(((f32[2,2,10,5120]{3,1,2,0:T(2,128)}), f32[16,2,10,5120]{3,1,2,0:T(2,128)}) %all-gather.4.cloned.1.call-update) | async-done | bytes 6553616 | tf_op jit(solution)/shard_map/all_gather | solution.py:94
  136.0 5.1 %gather_fusion = f32[2,2,10,5120]{3,1,2,0:T(2,128)} fusion(f32[16,2,10,5120]{3,1,2,0:T(2,128)} %all-gather.4.cloned.1.call-done, s32[1024]{0:T(1024)S(1)} %pad_clamp_fusion), kind=kCustom, calls=%fused_computation.clone | custom fusion | bytes 1638408 | tf_op jit(solution)/shard_map/jit(_take)/gather | solution.py:97
  141.1 1.6 fusion.2
  143.6 3.9 multiply_add_fusion.2
  147.6 1.3 collective-permute-start.6
  148.9 1.3 collective-permute-start.7
  150.2 3.6 collective-permute-done.7
  154.0 1.5 copy.62
  156.3 1.3 collective-permute-start.9
  157.6 6.3 %collective-permute-start.8 = (f32[1,2,10,5120]{3,1,2,0:T(2,128)S(1)}, f32[1,2,10,5120]{3,1,2,0:T(2,128)S(1)}, u32[]{:S(2)}, u32[]{:S(2)}) collective-permute-start(f32[1,2,10,5120]{3,1,2,0:T(2,128)S(1)} %copy.58), channel_id=1, source_target_pairs={{0,16},{16,32},{32,48},{48,64},{64,80},{80,96},{96,112},{1,17},{17... | collective-permute-start | bytes 1228808 | tf_op jit(solution)/shard_map/ppermute | solution.py:16
  163.9 1.3 fusion.107
  165.2 4.8 %collective-permute-done.9 = f32[1,2,10,5120]{3,1,2,0:T(2,128)S(1)} collective-permute-done((f32[1,2,10,5120]{3,1,2,0:T(2,128)S(1)}, f32[1,2,10,5120]{3,1,2,0:T(2,128)S(1)}, u32[]{:S(2)}, u32[]{:S(2)}) %collective-permute-start.9) | collective-permute-done | bytes 409632 | tf_op jit(solution)/shard_map/ppermute | solution.py:19
  170.1 16.5 %collective-permute-done.8 = f32[1,2,10,5120]{3,1,2,0:T(2,128)S(1)} collective-permute-done((f32[1,2,10,5120]{3,1,2,0:T(2,128)S(1)}, f32[1,2,10,5120]{3,1,2,0:T(2,128)S(1)}, u32[]{:S(2)}, u32[]{:S(2)}) %collective-permute-start.8) | collective-permute-done | bytes 409632 | tf_op jit(solution)/shard_map/ppermute | solution.py:16
  187.1 1.7 fusion.95
  188.8 1.5 fusion.96
  190.3 69.0 %all-gather.6.cloned.1.call-done = f32[16,2,10,5120]{3,1,2,0:T(2,128)} async-done(((f32[2,2,10,5120]{3,1,2,0:T(2,128)}), f32[16,2,10,5120]{3,1,2,0:T(2,128)}) %all-gather.6.cloned.1.call-update) | async-done | bytes 6553616 | tf_op jit(solution)/shard_map/all_gather | solution.py:94
  259.2 5.1 %gather_fusion.1 = f32[2,2,10,5120]{3,1,2,0:T(2,128)} fusion(f32[16,2,10,5120]{3,1,2,0:T(2,128)} %all-gather.6.cloned.1.call-done, s32[1024]{0:T(1024)S(1)} %pad_clamp_fusion), kind=kCustom, calls=%fused_computation.1.clone | custom fusion | bytes 1638408 | tf_op jit(solution)/shard_map/jit(_take)/gather | solution.py:97
  264.4 1.6 fusion.1
  266.9 3.9 multiply_add_fusion.1
  270.8 1.3 collective-permute-start.10
  272.1 1.3 collective-permute-start.11
  273.5 3.6 collective-permute-done.11
  277.3 1.5 copy.68
  279.5 1.3 collective-permute-start.13
  280.8 6.1 %collective-permute-start.12 = (f32[1,2,10,5120]{3,1,2,0:T(2,128)S(1)}, f32[1,2,10,5120]{3,1,2,0:T(2,128)S(1)}, u32[]{:S(2)}, u32[]{:S(2)}) collective-permute-start(f32[1,2,10,5120]{3,1,2,0:T(2,128)S(1)} %copy.64), channel_id=1, source_target_pairs={{0,16},{16,32},{32,48},{48,64},{64,80},{80,96},{96,112},{1,17},{17... | collective-permute-start | bytes 1228808 | tf_op jit(solution)/shard_map/ppermute | solution.py:16
  286.9 1.3 fusion.105
  288.2 5.0 %collective-permute-done.13 = f32[1,2,10,5120]{3,1,2,0:T(2,128)S(1)} collective-permute-done((f32[1,2,10,5120]{3,1,2,0:T(2,128)S(1)}, f32[1,2,10,5120]{3,1,2,0:T(2,128)S(1)}, u32[]{:S(2)}, u32[]{:S(2)}) %collective-permute-start.13) | collective-permute-done | bytes 409632 | tf_op jit(solution)/shard_map/ppermute | solution.py:19
  293.3 16.5 %collective-permute-done.12 = f32[1,2,10,5120]{3,1,2,0:T(2,128)S(1)} collective-permute-done((f32[1,2,10,5120]{3,1,2,0:T(2,128)S(1)}, f32[1,2,10,5120]{3,1,2,0:T(2,128)S(1)}, u32[]{:S(2)}, u32[]{:S(2)}) %collective-permute-start.12) | collective-permute-done | bytes 409632 | tf_op jit(solution)/shard_map/ppermute | solution.py:16
  310.3 1.8 fusion.93
  312.1 1.5 fusion.94
  313.6 68.8 %all-gather.8.cloned.1.call-done = f32[16,2,10,5120]{3,1,2,0:T(2,128)} async-done(((f32[2,2,10,5120]{3,1,2,0:T(2,128)}), f32[16,2,10,5120]{3,1,2,0:T(2,128)}) %all-gather.8.cloned.1.call-update) | async-done | bytes 6553616 | tf_op jit(solution)/shard_map/all_gather | solution.py:94
  382.5 4.4 %gather_fusion.2 = f32[2,2,10,5120]{3,1,2,0:T(2,128)S(1)} fusion(f32[16,2,10,5120]{3,1,2,0:T(2,128)} %all-gather.8.cloned.1.call-done, s32[1024]{0:T(1024)} %copy-done.49), kind=kCustom, calls=%fused_computation.2.clone | custom fusion | bytes 1638408 | tf_op jit(solution)/shard_map/jit(_take)/gather | solution.py:97
  389.2 4.1 %multiply_add_fusion = (f32[2,2,8,5120]{3,2,1,0:T(8,128)}, f32[2,2,8,5120]{3,2,1,0:T(8,128)}) fusion(f32[2,2,8,5120]{3,2,1,0:T(8,128)S(1)} %get-tuple-element.18, f32[2,2,8,5119]{3,2,1,0:T(8,128)S(1)} %get-tuple-element.39, f32[2]{0:T(128)S(1)} %get-tuple-element.86, f32[2,2,10,5120]{3,2,1,0:T(8,128)S(1)} %fusion, f32[2]{0:T(128)S(1)} %get-tuple-element.85, ...), kind=kLoop, calls=%fused_computation.132 | loop fusion | flops 8192000 | bytes 13925496 | tf_op jit(solution)/shard_map/add | solution.py:111
  (155 shorter events, 14.8 us)
Async XLA Ops:
  7.2 128.8 %all-gather.4.cloned.1.call-start = ((), (), s32[]{:S(2)}) async-start(), calls=%async_computation | async-start | bytes 7372800 | tf_op jit(solution)/shard_map/all_gather | solution.py:94
  8.6 10.5 %collective-permute-start.2 = (f32[2,2,1,5120]{3,2,1,0:T(1,128)S(1)}, f32[2,2,1,5120]{3,2,1,0:T(1,128)S(1)}, u32[]{:S(2)}, u32[]{:S(2)}) collective-permute-start(f32[2,2,1,5120]{3,2,1,0:T(1,128)S(1)} %get-tuple-element.72), channel_id=1, source_target_pairs={{0,1},{1,2},{2,3},{3,4},{4,5},{5,6},{6,7},{7,8},{8,9},{9,10},{10,1... | collective-permute-start | bytes 245768 | tf_op jit(solution)/shard_map/ppermute | solution.py:16
  9.9 9.2 %collective-permute-start.3 = (f32[2,2,1,5120]{3,2,1,0:T(1,128)S(1)}, f32[2,2,1,5120]{3,2,1,0:T(1,128)S(1)}, u32[]{:S(2)}, u32[]{:S(2)}) collective-permute-start(f32[2,2,1,5120]{3,2,1,0:T(1,128)S(1)} %get-tuple-element.73), channel_id=1, source_target_pairs={{1,0},{2,1},{3,2},{4,3},{5,4},{6,5},{7,6},{8,7},{9,8},{10,9},{11,1... | collective-permute-start | bytes 245768 | tf_op jit(solution)/shard_map/ppermute | solution.py:19
  20.5 8.1 %copy-start.50 = (s32[16]{0:T(128)S(1)}, s32[16]{0:T(128)}, u32[]{:S(2)}) copy-start(s32[16]{0:T(128)} %param.17) | copy-start | bytes 196
  20.5 8.1 %copy-start.32 = (f32[2,3]{1,0:T(2,128)S(1)}, f32[2,3]{1,0:T(2,128)}, u32[]{:S(2)}) copy-start(f32[2,3]{1,0:T(2,128)} %param.16) | copy-start | bytes 76
  20.5 8.3 %copy-start.31 = (f32[2,3,2]{1,2,0:T(2,128)S(1)}, f32[2,3,2]{1,2,0:T(2,128)}, u32[]{:S(2)}) copy-start(f32[2,3,2]{1,2,0:T(2,128)} %param.15) | copy-start | bytes 148
  20.5 8.6 %copy-start = (f32[2,2,8,5120]{3,2,1,0:T(8,128)S(1)}, f32[2,2,8,5120]{3,2,1,0:T(8,128)}, u32[]{:S(2)}) copy-start(f32[2,2,8,5120]{3,2,1,0:T(8,128)} %param.10) | copy-start | bytes 1966084
  22.1 237.2 %all-gather.6.cloned.1.call-start = ((), (), s32[]{:S(2)}) async-start(), calls=%async_computation.1 | async-start | bytes 7372800 | tf_op jit(solution)/shard_map/all_gather | solution.py:94
  22.3 8.1 %collective-permute-start = (f32[2,2,1,5120]{3,2,1,0:T(1,128)S(1)}, f32[2,2,1,5120]{3,2,1,0:T(1,128)S(1)}, u32[]{:S(2)}, u32[]{:S(2)}) collective-permute-start(f32[2,2,1,5120]{3,2,1,0:T(1,128)S(1)} %get-tuple-element.70), channel_id=1, source_target_pairs={{0,1},{1,2},{2,3},{3,4},{4,5},{5,6},{6,7},{7,8},{8,9},{9,10},{10,1... | collective-permute-start | bytes 245768 | tf_op jit(solution)/shard_map/ppermute | solution.py:16
  27.2 4.4 %collective-permute-start.1 = (f32[2,2,1,5120]{3,2,1,0:T(1,128)S(1)}, f32[2,2,1,5120]{3,2,1,0:T(1,128)S(1)}, u32[]{:S(2)}, u32[]{:S(2)}) collective-permute-start(f32[2,2,1,5120]{3,2,1,0:T(1,128)S(1)} %get-tuple-element.71), channel_id=1, source_target_pairs={{1,0},{2,1},{3,2},{4,3},{5,4},{6,5},{7,6},{8,7},{9,8},{10,9},{11,1... | collective-permute-start | bytes 245768 | tf_op jit(solution)/shard_map/ppermute | solution.py:19
  28.6 235.7 %copy-start.47 = (pred[2]{0:T(512)(128)(4,1)}, pred[2]{0:T(512)(128)(4,1)S(1)}, u32[]{:S(2)}) copy-start(pred[2]{0:T(512)(128)(4,1)S(1)} %get-tuple-element.22) | copy-start | bytes 10
  28.6 235.7 %copy-start.48 = (pred[2]{0:T(512)(128)(4,1)}, pred[2]{0:T(512)(128)(4,1)S(1)}, u32[]{:S(2)}) copy-start(pred[2]{0:T(512)(128)(4,1)S(1)} %get-tuple-element.96) | copy-start | bytes 10
  29.0 237.5 %copy-start.39 = (f32[2]{0:T(128)}, f32[2]{0:T(128)S(1)}, u32[]{:S(2)}) copy-start(f32[2]{0:T(128)S(1)} %get-tuple-element.76) | copy-start | bytes 28
  29.1 237.5 %copy-start.41 = (f32[2]{0:T(128)}, f32[2]{0:T(128)S(1)}, u32[]{:S(2)}) copy-start(f32[2]{0:T(128)S(1)} %get-tuple-element.77) | copy-start | bytes 28
  29.1 237.5 %copy-start.43 = (f32[2]{0:T(128)}, f32[2]{0:T(128)S(1)}, u32[]{:S(2)}) copy-start(f32[2]{0:T(128)S(1)} %get-tuple-element.78) | copy-start | bytes 28
  29.1 237.5 %copy-start.45 = (f32[2]{0:T(128)}, f32[2]{0:T(128)S(1)}, u32[]{:S(2)}) copy-start(f32[2]{0:T(128)S(1)} %get-tuple-element.79) | copy-start | bytes 28
  29.1 237.4 %copy-start.33 = (f32[2]{0:T(128)}, f32[2]{0:T(128)S(1)}, u32[]{:S(2)}) copy-start(f32[2]{0:T(128)S(1)} %get-tuple-element.98) | copy-start | bytes 28
  29.1 237.4 %copy-start.35 = (f32[2]{0:T(128)}, f32[2]{0:T(128)S(1)}, u32[]{:S(2)}) copy-start(f32[2]{0:T(128)S(1)} %get-tuple-element.99) | copy-start | bytes 28
  29.1 237.4 %copy-start.37 = (f32[2]{0:T(128)}, f32[2]{0:T(128)S(1)}, u32[]{:S(2)}) copy-start(f32[2]{0:T(128)S(1)} %get-tuple-element.100) | copy-start | bytes 28
  30.4 228.9 %copy-start.49 = (s32[1024]{0:T(1024)}, s32[1024]{0:T(1024)S(1)}, u32[]{:S(2)}) copy-start(s32[1024]{0:T(1024)S(1)} %pad_clamp_fusion) | copy-start | bytes 12292
  33.5 19.1 %collective-permute-start.5 = (f32[1,2,10,5120]{3,1,2,0:T(2,128)S(1)}, f32[1,2,10,5120]{3,1,2,0:T(2,128)S(1)}, u32[]{:S(2)}, u32[]{:S(2)}) collective-permute-start(f32[1,2,10,5120]{3,1,2,0:T(2,128)S(1)} %copy.54), channel_id=1, source_target_pairs={{16,0},{32,16},{48,32},{64,48},{80,64},{96,80},{112,96},{17,1},{33... | collective-permute-start | bytes 1228808 | tf_op jit(solution)/shard_map/ppermute | solution.py:19
  34.8 30.0 %collective-permute-start.4 = (f32[1,2,10,5120]{3,1,2,0:T(2,128)S(1)}, f32[1,2,10,5120]{3,1,2,0:T(2,128)S(1)}, u32[]{:S(2)}, u32[]{:S(2)}) collective-permute-start(f32[1,2,10,5120]{3,1,2,0:T(2,128)S(1)} %copy.52), channel_id=1, source_target_pairs={{0,16},{16,32},{32,48},{48,64},{64,80},{80,96},{96,112},{1,17},{17... | collective-permute-start | bytes 1228808 | tf_op jit(solution)/shard_map/ppermute | solution.py:16
  141.1 2.2 copy-start.19
  141.1 2.3 copy-start.22
  141.1 2.5 copy-start.27
  147.6 2.6 collective-permute-start.6
  148.9 4.9 %collective-permute-start.7 = (f32[2,2,1,5120]{3,2,1,0:T(1,128)S(1)}, f32[2,2,1,5120]{3,2,1,0:T(1,128)S(1)}, u32[]{:S(2)}, u32[]{:S(2)}) collective-permute-start(f32[2,2,1,5120]{3,2,1,0:T(1,128)S(1)} %get-tuple-element.63), channel_id=1, source_target_pairs={{1,0},{2,1},{3,2},{4,3},{5,4},{6,5},{7,6},{8,7},{9,8},{10,9},{11,1... | collective-permute-start | bytes 245768 | tf_op jit(solution)/shard_map/ppermute | solution.py:19
  155.5 226.9 %all-gather.8.cloned.1.call-start = ((), (), s32[]{:S(2)}) async-start(), calls=%async_computation.2 | async-start | bytes 7372800 | tf_op jit(solution)/shard_map/all_gather | solution.py:94
  156.3 13.6 %collective-permute-start.9 = (f32[1,2,10,5120]{3,1,2,0:T(2,128)S(1)}, f32[1,2,10,5120]{3,1,2,0:T(2,128)S(1)}, u32[]{:S(2)}, u32[]{:S(2)}) collective-permute-start(f32[1,2,10,5120]{3,1,2,0:T(2,128)S(1)} %copy.60), channel_id=1, source_target_pairs={{16,0},{32,16},{48,32},{64,48},{80,64},{96,80},{112,96},{17,1},{33... | collective-permute-start | bytes 1228808 | tf_op jit(solution)/shard_map/ppermute | solution.py:19
  157.6 29.0 %collective-permute-start.8 = (f32[1,2,10,5120]{3,1,2,0:T(2,128)S(1)}, f32[1,2,10,5120]{3,1,2,0:T(2,128)S(1)}, u32[]{:S(2)}, u32[]{:S(2)}) collective-permute-start(f32[1,2,10,5120]{3,1,2,0:T(2,128)S(1)} %copy.58), channel_id=1, source_target_pairs={{0,16},{16,32},{32,48},{48,64},{64,80},{80,96},{96,112},{1,17},{17... | collective-permute-start | bytes 1228808 | tf_op jit(solution)/shard_map/ppermute | solution.py:16
  264.4 2.2 copy-start.6
  264.4 2.2 copy-start.8
  264.4 2.2 copy-start.11
  264.4 2.2 copy-start.14
  264.4 2.2 copy-start.17
  264.4 2.2 copy-start.20
  264.4 2.3 copy-start.23
  264.4 2.5 copy-start.26
  270.8 2.6 collective-permute-start.10
  272.1 4.9 %collective-permute-start.11 = (f32[2,2,1,5120]{3,2,1,0:T(1,128)S(1)}, f32[2,2,1,5120]{3,2,1,0:T(1,128)S(1)}, u32[]{:S(2)}, u32[]{:S(2)}) collective-permute-start(f32[2,2,1,5120]{3,2,1,0:T(1,128)S(1)} %get-tuple-element.59), channel_id=1, source_target_pairs={{1,0},{2,1},{3,2},{4,3},{5,4},{6,5},{7,6},{8,7},{9,8},{10,9},{11,1... | collective-permute-start | bytes 245768 | tf_op jit(solution)/shard_map/ppermute | solution.py:19
  277.0 32.9 %copy-start.29 = (f32[2,2,1,5120]{3,2,1,0:T(1,128)}, f32[2,2,1,5120]{3,2,1,0:T(1,128)S(1)}, u32[]{:S(2)}) copy-start(f32[2,2,1,5120]{3,2,1,0:T(1,128)S(1)} %collective-permute-done.11) | copy-start | bytes 245764
  279.5 13.6 %collective-permute-start.13 = (f32[1,2,10,5120]{3,1,2,0:T(2,128)S(1)}, f32[1,2,10,5120]{3,1,2,0:T(2,128)S(1)}, u32[]{:S(2)}, u32[]{:S(2)}) collective-permute-start(f32[1,2,10,5120]{3,1,2,0:T(2,128)S(1)} %copy.66), channel_id=1, source_target_pairs={{16,0},{32,16},{48,32},{64,48},{80,64},{96,80},{112,96},{17,1},{33... | collective-permute-start | bytes 1228808 | tf_op jit(solution)/shard_map/ppermute | solution.py:19
  280.8 29.0 %collective-permute-start.12 = (f32[1,2,10,5120]{3,1,2,0:T(2,128)S(1)}, f32[1,2,10,5120]{3,1,2,0:T(2,128)S(1)}, u32[]{:S(2)}, u32[]{:S(2)}) collective-permute-start(f32[1,2,10,5120]{3,1,2,0:T(2,128)S(1)} %copy.64), channel_id=1, source_target_pairs={{0,16},{16,32},{32,48},{48,64},{64,80},{80,96},{96,112},{1,17},{17... | collective-permute-start | bytes 1228808 | tf_op jit(solution)/shard_map/ppermute | solution.py:16
  386.9 2.2 copy-start.25
  386.9 2.2 copy-start.30
  387.0 2.2 copy-start.34
  387.0 2.2 copy-start.36
  387.0 2.2 copy-start.38
  (20 other events, 38.6 us)
Sparse Core Ops, SparseCore 0:
  22.2 113.7 all-gather.3
  155.7 103.5 all-gather.5
  278.9 103.4 all-gather.7
where the time goes:
time: 401 us; the launch traced here: 400 us
  waiting for transfers between devices  277 us (69%)
  local copies, waits for them, and re-layouts  45.2 us (11%)
  starting transfers between devices  36.8 us (9%)
  other arithmetic  25.7 us (6%)
  between operations  14.7 us (4%)
    all_gather x3, waiting for transfers between devices, body(): piece = lax.all_gather(field_ext, 'gz', axis=0, tiled=True)  205 us
    ppermute x7, waiting for transfers between devices, extended(): lax.ppermute(lax.slice_in_dim(block, block.shape[dim] - width, None, axis...  45.1 us
    ppermute x7, starting transfers between devices, extended(): lax.ppermute(lax.slice_in_dim(block, block.shape[dim] - width, None, axis...  27.6 us
    ppermute x7, waiting for transfers between devices, extended(): lax.ppermute(lax.slice_in_dim(block, 0, width, axis=dim), axis, backward)  27.3 us
    gather x3, local copies, waits for them, and re-layouts, body(): chosen = jnp.take(piece, jnp.clip(wanted, 0, count - 1), axis=0)  14.6 us
    add x3, other arithmetic, body(): field = field_ext[:, :, 1:-1] + STEP * velocity  11.8 us
    slice x8, local copies, waits for them, and re-layouts, shift_left(): field[..., 1:]  9.89 us
    ppermute x7, starting transfers between devices, extended(): lax.ppermute(lax.slice_in_dim(block, 0, width, axis=dim), axis, backward)  9.04 us
  transfers between devices with their start and end apart: 17, of which 12 were waited for; matrix products, arithmetic and copies ran while one was open for 7% of the time, Pallas kernels for 0%

commit v1 on v0

--- a/solution.py
+++ b/solution.py
@@ -91,7 +91,9 @@
         field_ext = extended(field, (("tile", 2),), 1)
         vel_inner = velocity
         faces = extended(field_ext, (("gz", 0),), 1)
-        piece = lax.all_gather(field_ext, "gz", axis=0, tiled=True)
+        piece = jnp.concatenate(
+            lax.all_to_all(jnp.stack([field_ext] * lax.axis_size("gz")), "gz", 0, 0), axis=0
+        )
         count = piece.shape[0]
         inside = (wanted >= 0) & (wanted < count)
         chosen = jnp.take(piece, jnp.clip(wanted, 0, count - 1), axis=0)

time: 401 us -> 429 us (1.070)
  the two profiles are of different devices: /device:TPU:0 before, /device:TPU:31 now
where the time goes in v1:
time: 429 us; the launch traced here: 428 us
  waiting for transfers between devices  267 us (62%)
  starting transfers between devices  71.1 us (17%)
  local copies, waits for them, and re-layouts  60.7 us (14%)
  other arithmetic  28.2 us (7%)
    ppermute x7, waiting for transfers between devices, extended(): lax.ppermute(lax.slice_in_dim(block, block.shape[dim] - width, None, axis...  266 us
    ppermute x7, starting transfers between devices, extended(): lax.ppermute(lax.slice_in_dim(block, block.shape[dim] - width, None, axis...  34.8 us
    ppermute x7, starting transfers between devices, extended(): lax.ppermute(lax.slice_in_dim(block, 0, width, axis=dim), axis, backward)  19.4 us
    all_to_all x3, starting transfers between devices, body(): lax.all_to_all(jnp.stack([field_ext] * lax.axis_size('gz')), 'gz', 0, 0)  17 us
    another operation x3, local copies, waits for them, and re-layouts, body(): jnp.stack([field_ext] * lax.axis_size('gz'))  15.9 us
    gather x3, local copies, waits for them, and re-layouts, body(): chosen = jnp.take(piece, jnp.clip(wanted, 0, count - 1), axis=0)  15 us
    add x3, other arithmetic, body(): field = field_ext[:, :, 1:-1] + STEP * velocity  11.9 us
    slice x8, local copies, waits for them, and re-layouts, shift_left(): field[..., 1:]  9.28 us
  transfers between devices with their start and end apart: 17, of which 6 were waited for; matrix products, arithmetic and copies ran while one was open for 9% of the time, Pallas kernels for 0%

profile of v1, /device:TPU:31, one launch (start us, length us, event | category | flops | bytes accessed | tf_op | source)
XLA Modules:
  0.0 428.1 jit_solution(10808166296030221357)
XLA Ops:
  0.6 1.5 fusion.111
  2.1 2.6 collective-permute-start.3
  4.7 5.1 %collective-permute-start.2 = (f32[2,2,1,5120]{3,2,1,0:T(1,128)S(1)}, f32[2,2,1,5120]{3,2,1,0:T(1,128)S(1)}, u32[]{:S(2)}, u32[]{:S(2)}) collective-permute-start(f32[2,2,1,5120]{3,2,1,0:T(1,128)S(1)} %get-tuple-element.70), channel_id=1, source_target_pairs={{0,1},{1,2},{2,3},{3,4},{4,5},{5,6},{6,7},{7,8},{8,9},{9,10},{10,1... | collective-permute-start | bytes 245768 | tf_op jit(solution)/shard_map/ppermute | solution.py:16
  10.8 1.6 fusion.113
  12.4 6.4 %multiply_bitcast_fusion = f32[1,2,8,5120]{3,2,1,0:T(8,128)S(1)} fusion(s32[2,8,5120]{2,1,0:T(8,128)} %param.13, s32[2,8,5120]{2,1,0:T(8,128)} %param.12, f32[]{:T(128)} %bitcast.7, f32[]{:T(128)} %bitcast.6, f32[]{:T(128)} %bitcast.5, f32[]{:T(128)} %bitcast.4, f32[]{:T(128)} %bitcast.3, f32[]{:T(128)} %bitcast.2, f32[]{:T(128)} %bitcast.1, f32[]{:T(128)} %bitcast), kind=kLoop, calls=%fused_computation.137 | loop fusion | flops 1474560 | bytes 983072 | tf_op jit(solution)/shard_map/stack | solution.py:83
  19.0 1.9 collective-permute-start.1
  20.9 5.8 %collective-permute-start = (f32[2,2,1,5120]{3,2,1,0:T(1,128)S(1)}, f32[2,2,1,5120]{3,2,1,0:T(1,128)S(1)}, u32[]{:S(2)}, u32[]{:S(2)}) collective-permute-start(f32[2,2,1,5120]{3,2,1,0:T(1,128)S(1)} %get-tuple-element.68), channel_id=1, source_target_pairs={{0,1},{1,2},{2,3},{3,4},{4,5},{5,6},{6,7},{7,8},{8,9},{9,10},{10,1... | collective-permute-start | bytes 245768 | tf_op jit(solution)/shard_map/ppermute | solution.py:16
  26.7 1.3 fusion.110
  31.7 5.3 %stack.15 = f32[8,2,2,10,5120]{4,2,3,1,0:T(2,128)} broadcast(f32[2,2,10,5120]{3,1,2,0:T(2,128)S(1)} %copy.38), dimensions={1,2,3,4} | broadcast | bytes 7372800 | tf_op jit(solution)/shard_map/stack | solution.py:95
  37.0 7.5 %all-to-all-start = ((f32[8,2,2,10,5120]{4,2,3,1,0:T(2,128)}), f32[8,2,2,10,5120]{4,2,3,1,0:T(2,128)}, u32[]{:S(2)}, u32[]{:S(2)}) async-start(f32[8,2,2,10,5120]{4,2,3,1,0:T(2,128)} %stack.15), calls=%async_computation | async-start | bytes 13107200 | tf_op jit(solution)/shard_map/all_to_all | solution.py:95
  44.9 4.6 %collective-permute-start.4 = (f32[1,2,10,5120]{3,1,2,0:T(2,128)S(1)}, f32[1,2,10,5120]{3,1,2,0:T(2,128)S(1)}, u32[]{:S(2)}, u32[]{:S(2)}) collective-permute-start(f32[1,2,10,5120]{3,1,2,0:T(2,128)S(1)} %copy.34), channel_id=1, source_target_pairs={{0,16},{16,32},{32,48},{48,64},{64,80},{80,96},{96,112},{1,17},{17... | collective-permute-start | bytes 1228808 | tf_op jit(solution)/shard_map/ppermute | solution.py:16
  49.8 3.1 collective-permute-start.5
  56.2 84.7 %collective-permute-done.4 = f32[1,2,10,5120]{3,1,2,0:T(2,128)S(1)} collective-permute-done((f32[1,2,10,5120]{3,1,2,0:T(2,128)S(1)}, f32[1,2,10,5120]{3,1,2,0:T(2,128)S(1)}, u32[]{:S(2)}, u32[]{:S(2)}) %collective-permute-start.4) | collective-permute-done | bytes 409632 | tf_op jit(solution)/shard_map/ppermute | solution.py:16
  141.5 1.3 copy-done.3
  142.8 2.2 fusion.97
  145.0 5.3 %gather_fusion = f32[2,2,10,5120]{3,1,2,0:T(2,128)} fusion(f32[16,2,10,5120]{3,1,2,0:T(2,128)} %bitcast.15, s32[1024]{0:T(1024)} %pad_clamp_fusion), kind=kCustom, calls=%fused_computation.clone | custom fusion | bytes 1638408 | tf_op jit(solution)/shard_map/jit(_take)/gather | solution.py:99
  150.4 1.6 fusion.2
  152.9 4.0 multiply_add_fusion.2
  156.9 1.9 collective-permute-start.7
  158.9 5.9 %collective-permute-start.6 = (f32[2,2,1,5120]{3,2,1,0:T(1,128)S(1)}, f32[2,2,1,5120]{3,2,1,0:T(1,128)S(1)}, u32[]{:S(2)}, u32[]{:S(2)}) collective-permute-start(f32[2,2,1,5120]{3,2,1,0:T(1,128)S(1)} %get-tuple-element.60), channel_id=1, source_target_pairs={{0,1},{1,2},{2,3},{3,4},{4,5},{5,6},{6,7},{7,8},{8,9},{9,10},{10,1... | collective-permute-start | bytes 245768 | tf_op jit(solution)/shard_map/ppermute | solution.py:16
  164.8 1.3 collective-permute-done.6
  167.0 5.3 %stack.16 = f32[8,2,2,10,5120]{4,2,3,1,0:T(2,128)} broadcast(f32[2,2,10,5120]{3,1,2,0:T(2,128)S(1)} %copy.44), dimensions={1,2,3,4} | broadcast | bytes 7372800 | tf_op jit(solution)/shard_map/stack | solution.py:95
  172.3 4.7 %all-to-all-start.1 = ((f32[8,2,2,10,5120]{4,2,3,1,0:T(2,128)}), f32[8,2,2,10,5120]{4,2,3,1,0:T(2,128)}, u32[]{:S(2)}, u32[]{:S(2)}) async-start(f32[8,2,2,10,5120]{4,2,3,1,0:T(2,128)} %stack.16), calls=%async_computation.1 | async-start | bytes 13107200 | tf_op jit(solution)/shard_map/all_to_all | solution.py:95
  177.4 4.0 collective-permute-start.8
  181.8 3.7 collective-permute-start.9
  185.4 1.3 fusion.107
  186.7 89.8 %collective-permute-done.8 = f32[1,2,10,5120]{3,1,2,0:T(2,128)S(1)} collective-permute-done((f32[1,2,10,5120]{3,1,2,0:T(2,128)S(1)}, f32[1,2,10,5120]{3,1,2,0:T(2,128)S(1)}, u32[]{:S(2)}, u32[]{:S(2)}) %collective-permute-start.8) | collective-permute-done | bytes 409632 | tf_op jit(solution)/shard_map/ppermute | solution.py:16
  277.2 1.3 copy-done.5
  278.5 1.5 fusion.96
  279.9 1.5 fusion.95
  281.4 5.3 %gather_fusion.1 = f32[2,2,10,5120]{3,1,2,0:T(2,128)} fusion(f32[16,2,10,5120]{3,1,2,0:T(2,128)} %bitcast.16, s32[1024]{0:T(1024)} %pad_clamp_fusion), kind=kCustom, calls=%fused_computation.1.clone | custom fusion | bytes 1638408 | tf_op jit(solution)/shard_map/jit(_take)/gather | solution.py:99
  286.8 1.6 fusion.1
  289.2 3.9 multiply_add_fusion.1
  293.2 2.3 collective-permute-start.11
  295.5 5.4 %collective-permute-start.10 = (f32[2,2,1,5120]{3,2,1,0:T(1,128)S(1)}, f32[2,2,1,5120]{3,2,1,0:T(1,128)S(1)}, u32[]{:S(2)}, u32[]{:S(2)}) collective-permute-start(f32[2,2,1,5120]{3,2,1,0:T(1,128)S(1)} %get-tuple-element.56), channel_id=1, source_target_pairs={{0,1},{1,2},{2,3},{3,4},{4,5},{5,6},{6,7},{7,8},{8,9},{9,10},{10,1... | collective-permute-start | bytes 245768 | tf_op jit(solution)/shard_map/ppermute | solution.py:16
  301.1 1.3 collective-permute-done.10
  303.2 5.3 %stack.17 = f32[8,2,2,10,5120]{4,2,3,1,0:T(2,128)} broadcast(f32[2,2,10,5120]{3,1,2,0:T(2,128)S(1)} %copy.50), dimensions={1,2,3,4} | broadcast | bytes 7372800 | tf_op jit(solution)/shard_map/stack | solution.py:95
  308.5 4.7 %all-to-all-start.2 = ((f32[8,2,2,10,5120]{4,2,3,1,0:T(2,128)}), f32[8,2,2,10,5120]{4,2,3,1,0:T(2,128)}, u32[]{:S(2)}, u32[]{:S(2)}) async-start(f32[8,2,2,10,5120]{4,2,3,1,0:T(2,128)} %stack.17), calls=%async_computation.2 | async-start | bytes 13107200 | tf_op jit(solution)/shard_map/all_to_all | solution.py:95
  313.7 4.0 collective-permute-start.12
  318.1 3.9 collective-permute-start.13
  322.0 1.3 fusion.105
  323.2 89.2 %collective-permute-done.12 = f32[1,2,10,5120]{3,1,2,0:T(2,128)S(1)} collective-permute-done((f32[1,2,10,5120]{3,1,2,0:T(2,128)S(1)}, f32[1,2,10,5120]{3,1,2,0:T(2,128)S(1)}, u32[]{:S(2)}, u32[]{:S(2)}) %collective-permute-start.12) | collective-permute-done | bytes 409632 | tf_op jit(solution)/shard_map/ppermute | solution.py:16
  413.1 1.3 copy-done.1
  414.4 1.5 fusion.94
  415.9 1.4 fusion.93
  417.3 4.4 %gather_fusion.2 = f32[2,2,10,5120]{3,1,2,0:T(2,128)S(1)} fusion(f32[16,2,10,5120]{3,1,2,0:T(2,128)} %bitcast.17, s32[1024]{0:T(1024)} %pad_clamp_fusion), kind=kCustom, calls=%fused_computation.2.clone | custom fusion | bytes 1638408 | tf_op jit(solution)/shard_map/jit(_take)/gather | solution.py:99
  421.9 1.2 fusion
  424.1 4.1 multiply_add_fusion
  (151 shorter events, 16.6 us)
Async XLA Ops:
  0.6 26.1 %copy-start = (f32[2,2,8,5120]{3,2,1,0:T(8,128)S(1)}, f32[2,2,8,5120]{3,2,1,0:T(8,128)}, u32[]{:S(2)}) copy-start(f32[2,2,8,5120]{3,2,1,0:T(8,128)} %param.10) | copy-start | bytes 1966084
  2.1 28.7 %collective-permute-start.3 = (f32[2,2,1,5120]{3,2,1,0:T(1,128)S(1)}, f32[2,2,1,5120]{3,2,1,0:T(1,128)S(1)}, u32[]{:S(2)}, u32[]{:S(2)}) collective-permute-start(f32[2,2,1,5120]{3,2,1,0:T(1,128)S(1)} %get-tuple-element.71), channel_id=1, source_target_pairs={{1,0},{2,1},{3,2},{4,3},{5,4},{6,5},{7,6},{8,7},{9,8},{10,9},{11,1... | collective-permute-start | bytes 245768 | tf_op jit(solution)/shard_map/ppermute | solution.py:19
  4.7 26.1 %collective-permute-start.2 = (f32[2,2,1,5120]{3,2,1,0:T(1,128)S(1)}, f32[2,2,1,5120]{3,2,1,0:T(1,128)S(1)}, u32[]{:S(2)}, u32[]{:S(2)}) collective-permute-start(f32[2,2,1,5120]{3,2,1,0:T(1,128)S(1)} %get-tuple-element.70), channel_id=1, source_target_pairs={{0,1},{1,2},{2,3},{3,4},{4,5},{5,6},{6,7},{7,8},{8,9},{9,10},{10,1... | collective-permute-start | bytes 245768 | tf_op jit(solution)/shard_map/ppermute | solution.py:16
  18.9 9.1 %copy-start.30 = (f32[2,3,2]{1,2,0:T(2,128)S(1)}, f32[2,3,2]{1,2,0:T(2,128)}, u32[]{:S(2)}) copy-start(f32[2,3,2]{1,2,0:T(2,128)} %param.15) | copy-start | bytes 148
  18.9 9.3 %copy-start.31 = (f32[2,3]{1,0:T(2,128)S(1)}, f32[2,3]{1,0:T(2,128)}, u32[]{:S(2)}) copy-start(f32[2,3]{1,0:T(2,128)} %param.16) | copy-start | bytes 76
  18.9 9.5 %copy-start.48 = (s32[16]{0:T(128)S(1)}, s32[16]{0:T(128)}, u32[]{:S(2)}) copy-start(s32[16]{0:T(128)} %param.17) | copy-start | bytes 196
  19.0 33.9 %collective-permute-start.1 = (f32[2,2,1,5120]{3,2,1,0:T(1,128)S(1)}, f32[2,2,1,5120]{3,2,1,0:T(1,128)S(1)}, u32[]{:S(2)}, u32[]{:S(2)}) collective-permute-start(f32[2,2,1,5120]{3,2,1,0:T(1,128)S(1)} %get-tuple-element.69), channel_id=1, source_target_pairs={{1,0},{2,1},{3,2},{4,3},{5,4},{6,5},{7,6},{8,7},{9,8},{10,9},{11,1... | collective-permute-start | bytes 245768 | tf_op jit(solution)/shard_map/ppermute | solution.py:19
  20.9 32.0 %collective-permute-start = (f32[2,2,1,5120]{3,2,1,0:T(1,128)S(1)}, f32[2,2,1,5120]{3,2,1,0:T(1,128)S(1)}, u32[]{:S(2)}, u32[]{:S(2)}) collective-permute-start(f32[2,2,1,5120]{3,2,1,0:T(1,128)S(1)} %get-tuple-element.68), channel_id=1, source_target_pairs={{0,1},{1,2},{2,3},{3,4},{4,5},{5,6},{6,7},{7,8},{8,9},{9,10},{10,1... | collective-permute-start | bytes 245768 | tf_op jit(solution)/shard_map/ppermute | solution.py:16
  37.0 108.0 %all-to-all-start = ((f32[8,2,2,10,5120]{4,2,3,1,0:T(2,128)}), f32[8,2,2,10,5120]{4,2,3,1,0:T(2,128)}, u32[]{:S(2)}, u32[]{:S(2)}) async-start(f32[8,2,2,10,5120]{4,2,3,1,0:T(2,128)} %stack.15), calls=%async_computation | async-start | bytes 13107200 | tf_op jit(solution)/shard_map/all_to_all | solution.py:95
  44.9 95.9 %collective-permute-start.4 = (f32[1,2,10,5120]{3,1,2,0:T(2,128)S(1)}, f32[1,2,10,5120]{3,1,2,0:T(2,128)S(1)}, u32[]{:S(2)}, u32[]{:S(2)}) collective-permute-start(f32[1,2,10,5120]{3,1,2,0:T(2,128)S(1)} %copy.34), channel_id=1, source_target_pairs={{0,16},{16,32},{32,48},{48,64},{64,80},{80,96},{96,112},{1,17},{17... | collective-permute-start | bytes 1228808 | tf_op jit(solution)/shard_map/ppermute | solution.py:16
  49.8 91.2 %collective-permute-start.5 = (f32[1,2,10,5120]{3,1,2,0:T(2,128)S(1)}, f32[1,2,10,5120]{3,1,2,0:T(2,128)S(1)}, u32[]{:S(2)}, u32[]{:S(2)}) collective-permute-start(f32[1,2,10,5120]{3,1,2,0:T(2,128)S(1)} %copy.36), channel_id=1, source_target_pairs={{16,0},{32,16},{48,32},{64,48},{80,64},{96,80},{112,96},{17,1},{33... | collective-permute-start | bytes 1228808 | tf_op jit(solution)/shard_map/ppermute | solution.py:19
  145.0 5.3 %copy-start.46 = (pred[2]{0:T(512)(128)(4,1)S(1)}, pred[2]{0:T(512)(128)(4,1)}, u32[]{:S(2)}) copy-start(pred[2]{0:T(512)(128)(4,1)} %get-tuple-element.20) | copy-start | bytes 10
  145.0 5.3 %copy-start.47 = (pred[2]{0:T(512)(128)(4,1)S(1)}, pred[2]{0:T(512)(128)(4,1)}, u32[]{:S(2)}) copy-start(pred[2]{0:T(512)(128)(4,1)} %get-tuple-element.94) | copy-start | bytes 10
  150.3 2.2 copy-start.4
  150.3 2.2 copy-start.7
  150.3 2.2 copy-start.10
  150.3 2.2 copy-start.13
  150.3 2.2 copy-start.16
  150.3 2.2 copy-start.19
  150.4 2.3 copy-start.22
  150.4 2.5 copy-start.27
  150.4 2.5 copy-start.32
  150.4 2.4 copy-start.34
  150.4 2.4 copy-start.36
  150.4 2.4 copy-start.38
  150.4 2.4 copy-start.40
  150.4 2.4 copy-start.42
  150.4 2.4 copy-start.44
  156.9 7.9 %collective-permute-start.7 = (f32[2,2,1,5120]{3,2,1,0:T(1,128)S(1)}, f32[2,2,1,5120]{3,2,1,0:T(1,128)S(1)}, u32[]{:S(2)}, u32[]{:S(2)}) collective-permute-start(f32[2,2,1,5120]{3,2,1,0:T(1,128)S(1)} %get-tuple-element.61), channel_id=1, source_target_pairs={{1,0},{2,1},{3,2},{4,3},{5,4},{6,5},{7,6},{8,7},{9,8},{10,9},{11,1... | collective-permute-start | bytes 245768 | tf_op jit(solution)/shard_map/ppermute | solution.py:19
  158.9 7.2 %collective-permute-start.6 = (f32[2,2,1,5120]{3,2,1,0:T(1,128)S(1)}, f32[2,2,1,5120]{3,2,1,0:T(1,128)S(1)}, u32[]{:S(2)}, u32[]{:S(2)}) collective-permute-start(f32[2,2,1,5120]{3,2,1,0:T(1,128)S(1)} %get-tuple-element.60), channel_id=1, source_target_pairs={{0,1},{1,2},{2,3},{3,4},{4,5},{5,6},{6,7},{7,8},{8,9},{9,10},{10,1... | collective-permute-start | bytes 245768 | tf_op jit(solution)/shard_map/ppermute | solution.py:16
  172.3 109.2 %all-to-all-start.1 = ((f32[8,2,2,10,5120]{4,2,3,1,0:T(2,128)}), f32[8,2,2,10,5120]{4,2,3,1,0:T(2,128)}, u32[]{:S(2)}, u32[]{:S(2)}) async-start(f32[8,2,2,10,5120]{4,2,3,1,0:T(2,128)} %stack.16), calls=%async_computation.1 | async-start | bytes 13107200 | tf_op jit(solution)/shard_map/all_to_all | solution.py:95
  177.4 99.1 %collective-permute-start.8 = (f32[1,2,10,5120]{3,1,2,0:T(2,128)S(1)}, f32[1,2,10,5120]{3,1,2,0:T(2,128)S(1)}, u32[]{:S(2)}, u32[]{:S(2)}) collective-permute-start(f32[1,2,10,5120]{3,1,2,0:T(2,128)S(1)} %copy.40), channel_id=1, source_target_pairs={{0,16},{16,32},{32,48},{48,64},{64,80},{80,96},{96,112},{1,17},{17... | collective-permute-start | bytes 1228808 | tf_op jit(solution)/shard_map/ppermute | solution.py:16
  181.8 94.9 %collective-permute-start.9 = (f32[1,2,10,5120]{3,1,2,0:T(2,128)S(1)}, f32[1,2,10,5120]{3,1,2,0:T(2,128)S(1)}, u32[]{:S(2)}, u32[]{:S(2)}) collective-permute-start(f32[1,2,10,5120]{3,1,2,0:T(2,128)S(1)} %copy.42), channel_id=1, source_target_pairs={{16,0},{32,16},{48,32},{64,48},{80,64},{96,80},{112,96},{17,1},{33... | collective-permute-start | bytes 1228808 | tf_op jit(solution)/shard_map/ppermute | solution.py:19
  286.7 2.2 copy-start.20
  286.7 2.3 copy-start.23
  286.8 2.5 copy-start.26
  293.2 7.9 %collective-permute-start.11 = (f32[2,2,1,5120]{3,2,1,0:T(1,128)S(1)}, f32[2,2,1,5120]{3,2,1,0:T(1,128)S(1)}, u32[]{:S(2)}, u32[]{:S(2)}) collective-permute-start(f32[2,2,1,5120]{3,2,1,0:T(1,128)S(1)} %get-tuple-element.57), channel_id=1, source_target_pairs={{1,0},{2,1},{3,2},{4,3},{5,4},{6,5},{7,6},{8,7},{9,8},{10,9},{11,1... | collective-permute-start | bytes 245768 | tf_op jit(solution)/shard_map/ppermute | solution.py:19
  295.5 6.8 %collective-permute-start.10 = (f32[2,2,1,5120]{3,2,1,0:T(1,128)S(1)}, f32[2,2,1,5120]{3,2,1,0:T(1,128)S(1)}, u32[]{:S(2)}, u32[]{:S(2)}) collective-permute-start(f32[2,2,1,5120]{3,2,1,0:T(1,128)S(1)} %get-tuple-element.56), channel_id=1, source_target_pairs={{0,1},{1,2},{2,3},{3,4},{4,5},{5,6},{6,7},{7,8},{8,9},{9,10},{10,1... | collective-permute-start | bytes 245768 | tf_op jit(solution)/shard_map/ppermute | solution.py:16
  302.4 110.4 %copy-start.28 = (f32[2,2,1,5120]{3,2,1,0:T(1,128)}, f32[2,2,1,5120]{3,2,1,0:T(1,128)S(1)}, u32[]{:S(2)}) copy-start(f32[2,2,1,5120]{3,2,1,0:T(1,128)S(1)} %collective-permute-done.10) | copy-start | bytes 245764
  308.5 108.8 %all-to-all-start.2 = ((f32[8,2,2,10,5120]{4,2,3,1,0:T(2,128)}), f32[8,2,2,10,5120]{4,2,3,1,0:T(2,128)}, u32[]{:S(2)}, u32[]{:S(2)}) async-start(f32[8,2,2,10,5120]{4,2,3,1,0:T(2,128)} %stack.17), calls=%async_computation.2 | async-start | bytes 13107200 | tf_op jit(solution)/shard_map/all_to_all | solution.py:95
  313.7 98.8 %collective-permute-start.12 = (f32[1,2,10,5120]{3,1,2,0:T(2,128)S(1)}, f32[1,2,10,5120]{3,1,2,0:T(2,128)S(1)}, u32[]{:S(2)}, u32[]{:S(2)}) collective-permute-start(f32[1,2,10,5120]{3,1,2,0:T(2,128)S(1)} %copy.46), channel_id=1, source_target_pairs={{0,16},{16,32},{32,48},{48,64},{64,80},{80,96},{96,112},{1,17},{17... | collective-permute-start | bytes 1228808 | tf_op jit(solution)/shard_map/ppermute | solution.py:16
  318.1 94.5 %collective-permute-start.13 = (f32[1,2,10,5120]{3,1,2,0:T(2,128)S(1)}, f32[1,2,10,5120]{3,1,2,0:T(2,128)S(1)}, u32[]{:S(2)}, u32[]{:S(2)}) collective-permute-start(f32[1,2,10,5120]{3,1,2,0:T(2,128)S(1)} %copy.48), channel_id=1, source_target_pairs={{16,0},{32,16},{48,32},{64,48},{80,64},{96,80},{112,96},{17,1},{33... | collective-permute-start | bytes 1228808 | tf_op jit(solution)/shard_map/ppermute | solution.py:19
  421.8 2.2 copy-start.25
  421.8 2.2 copy-start.29
  421.8 2.2 copy-start.33
  421.8 2.2 copy-start.35
  421.8 2.2 copy-start.37
  421.8 2.2 copy-start.39
  (18 other events, 33.7 us)
